TPU v7x, 512 devices: a whole 4x4x16 slice. The times are simulated.
512 devices in a mesh: dp: 2 (over z_hi), row: 8 (over y, core), col: 32 (over x, z_lo).
Axes of the slice: x: 4, y: 4, z: 16 (z_hi: 2, z_lo: 8; z = z_hi * 8 + z_lo), core: 2. Of those that a mesh axis runs over, the one named last changes fastest.
Arguments:
- activations: bfloat16 [2048, 16384], P(('dp', 'row'), 'col'), may hold values from -6 to 6
- cotangent: bfloat16 [2048, 16384], P(('dp', 'row'), 'col'), may hold values from -6 to 6
- gate_saved: bfloat16 [2048, 6656], P(('dp', 'col'), 'row'), may hold values from -6 to 6
- up_saved: bfloat16 [2048, 6656], P(('dp', 'col'), 'row'), may hold values from -6 to 6
- w_gate: bfloat16 [16384, 6656], P('col', 'row'), may hold values from -0.046875 to 0.046875
- w_up: bfloat16 [16384, 6656], P('col', 'row'), may hold values from -0.046875 to 0.046875
- w_down: bfloat16 [6656, 16384], P('row', 'col'), may hold values from -0.078125 to 0.078125
- assignment: int32 [4], replicated, may hold values from 0 to 3, each once
- pair_lengths: int32 [8], replicated, may hold values from 1 to 256, 1536 in all
Outputs:
- input_grad: bfloat16 [2048, 16384], P(('dp', 'row'), 'col')
- gate_grad: bfloat16 [16384, 6656], P(('col', 'dp'), 'row')
- up_grad: bfloat16 [16384, 6656], P(('col', 'dp'), 'row')
- down_grad: bfloat16 [6656, 16384], P(('row', 'dp'), 'col')
Inputs may be any that keep to these rules, and one draw needn't show every extreme that they name: `assignment`: each of the 4 pairs stands in exactly one pair slot; pair slot s belongs to batch s // 2. `pair_lengths`: entry 2 p is the live length of pair p's chosen sequence and entry 2 p + 1 that of its rejected one; the largest entry is exactly 256.
All inputs are finite; a program needn't handle non-finite values.
Results may differ from a plain program's by a relative error of at most 0.019.
Values may be sent and summed in bfloat16 or wider, within the bound.
No kernel may reach another device: no remote copies, remote signals or barrier semaphores. Data moves between devices by JAX's collectives and lax.ppermute only.
A program may use at most 64 MiB of HBM per device.

v0:
```python
import jax
import jax.numpy as jnp
from jax import lax
from jax.sharding import PartitionSpec as P

SEQ = 256


def contract_last(left, right):
    return lax.dot_general(
        left, right, (((1,), (1,)), ((), ())), preferred_element_type=jnp.float32
    )


def contract_first(left, right):
    return lax.dot_general(
        left, right, (((0,), (0,)), ((), ())), preferred_element_type=jnp.float32
    )


def live_mask(assignment, pair_lengths, batch_id, row_count):
    seq_count = row_count // SEQ
    seq_index = jnp.arange(seq_count, dtype=jnp.int32)
    slot_ids = batch_id * (seq_count // 2) + seq_index // 2
    slot_table = jnp.arange(assignment.shape[0], dtype=jnp.int32)
    pair_ids = jnp.sum(
        jnp.where(slot_table[None, :] == slot_ids[:, None], assignment[None, :], 0), axis=1
    )
    entry_ids = 2 * pair_ids + seq_index % 2
    entry_table = jnp.arange(pair_lengths.shape[0], dtype=jnp.int32)
    live_len = jnp.sum(
        jnp.where(entry_table[None, :] == entry_ids[:, None], pair_lengths[None, :], 0), axis=1
    )
    position = jnp.arange(row_count, dtype=jnp.int32)
    return position % SEQ < jnp.repeat(live_len, SEQ, total_repeat_length=row_count)


def swiglu_grads(head_grad, gate_vals, up_vals):
    gate_float = gate_vals.astype(jnp.float32)
    up_float = up_vals.astype(jnp.float32)
    sigmoid_gate = jax.nn.sigmoid(gate_float)
    silu_gate = gate_float * sigmoid_gate
    hidden = (silu_gate * up_float).astype(jnp.bfloat16)
    grad_gate = (
        head_grad * up_float * sigmoid_gate * (1.0 + gate_float * (1.0 - sigmoid_gate))
    ).astype(jnp.bfloat16)
    grad_up = (head_grad * silu_gate).astype(jnp.bfloat16)
    return (grad_gate, grad_up, hidden)


def on_device(
    activations, cotangent, gate_saved, up_saved, w_gate, w_up, w_down, assignment, pair_lengths
):
    input_rows, output_grads = (
        lax.all_gather(activations, "row", axis=0, tiled=True),
        lax.all_gather(cotangent, "row", axis=0, tiled=True),
    )
    row_count = input_rows.shape[0]
    batch_id = lax.axis_index("dp")
    live_tokens = live_mask(assignment, pair_lengths, batch_id, row_count)
    masked = jnp.where(live_tokens[:, None], output_grads, jnp.zeros_like(output_grads))
    col_count = lax.axis_size("col")
    head_count = row_count // col_count
    block_term = contract_last(masked, w_down).astype(jnp.bfloat16)
    received = lax.all_to_all(block_term, "col", split_axis=0, concat_axis=0, tiled=True)
    stacked = received.reshape(col_count, head_count, received.shape[1])
    head_grad = jnp.sum(stacked, axis=0, dtype=jnp.float32)
    part_gate, part_up, part_hidden = swiglu_grads(head_grad, gate_saved, up_saved)
    grad_gate, grad_up, hidden = (
        lax.all_gather(part_gate, "col", axis=0, tiled=True),
        lax.all_gather(part_up, "col", axis=0, tiled=True),
        lax.all_gather(part_hidden, "col", axis=0, tiled=True),
    )
    input_grad = lax.psum_scatter(
        (contract_last(grad_gate, w_gate) + contract_last(grad_up, w_up)).astype(jnp.bfloat16),
        "row",
        scatter_dimension=0,
        tiled=True,
    )
    grad_scale = 1.0 / jnp.sqrt(jnp.float32(row_count * lax.axis_size("dp")))
    gate_term = contract_first(input_rows, grad_gate) * grad_scale
    up_term = contract_first(input_rows, grad_up) * grad_scale
    down_term = contract_first(hidden, masked) * grad_scale
    gate_total, up_total, down_total = (
        lax.psum_scatter(
            gate_term.astype(jnp.bfloat16), "dp", scatter_dimension=0, tiled=True
        ).astype(jnp.float32),
        lax.psum_scatter(
            up_term.astype(jnp.bfloat16), "dp", scatter_dimension=0, tiled=True
        ).astype(jnp.float32),
        lax.psum_scatter(
            down_term.astype(jnp.bfloat16), "dp", scatter_dimension=0, tiled=True
        ).astype(jnp.float32),
    )
    return (
        input_grad,
        gate_total.astype(jnp.bfloat16),
        up_total.astype(jnp.bfloat16),
        down_total.astype(jnp.bfloat16),
    )


def solution(mesh):
    return jax.shard_map(
        on_device,
        mesh=mesh,
        in_specs=(
            P(("dp", "row"), "col"),
            P(("dp", "row"), "col"),
            P(("dp", "col"), "row"),
            P(("dp", "col"), "row"),
            P("col", "row"),
            P("col", "row"),
            P("row", "col"),
            P(),
            P(),
        ),
        out_specs=(
            P(("dp", "row"), "col"),
            P(("col", "dp"), "row"),
            P(("col", "dp"), "row"),
            P(("row", "dp"), "col"),
        ),
        check_vma=False,
    )
```

profile of v0, /device:TPU:2, one launch (start us, length us, event | category | flops | bytes accessed | tf_op | source)
XLA Modules:
  0.0 1084.4 jit_solution(2719218604420227594)
XLA Ops:
  7.2 0.7 all-gather.6.cloned.1.call-update
  8.0 0.8 select_reduce_fusion.1
  8.8 0.8 select_reduce_fusion
  9.7 0.6 fusion.18
  10.3 3.3 fusion.10
  13.6 32.0 %all-gather.6.cloned.1.call-done = bf16[1024,512]{1,0:T(8,128)(2,1)} async-done(((bf16[128,512]{1,0:T(8,128)(2,1)}), bf16[1024,512]{1,0:T(8,128)(2,1)}) %all-gather.6.cloned.1.call-update) | async-done | bytes 1048592 | tf_op jit(solution)/shard_map/all_gather | solution.py:56
  45.6 3.6 convolution_convert_fusion
  49.1 3.0 copy.14
  52.2 95.9 %all_to_all.9 = bf16[32,32,832]{2,1,0:T(8,128)(2,1)S(1)} all-to-all(bf16[32,32,832]{2,1,0:T(8,128)(2,1)S(1)} %bitcast.19), channel_id=1, replica_groups=mesh['dp'=2,'row'=8,'col'=32] {'col'}, dimensions={0} | all-to-all | bytes 3407872 | tf_op jit(solution)/shard_map/all_to_all | solution.py:65
  148.9 0.7 multiply_convert_fusion.3
  149.7 0.7 all-gather.12.cloned.1.call-update
  151.6 199.6 %all-gather.14.cloned.1.call-done = bf16[1024,832]{1,0:T(8,128)(2,1)} async-done(((bf16[32,832]{1,0:T(8,128)(2,1)}), bf16[1024,832]{1,0:T(8,128)(2,1)}) %all-gather.14.cloned.1.call-update) | async-done | bytes 1703952 | tf_op jit(solution)/shard_map/all_gather | solution.py:72
  351.2 3.5 multiply_convert_fusion
  354.8 45.7 %all-gather.12.cloned.1.call-done = bf16[1024,512]{1,0:T(8,128)(2,1)} async-done(((bf16[128,512]{1,0:T(8,128)(2,1)}), bf16[1024,512]{1,0:T(8,128)(2,1)}) %all-gather.12.cloned.1.call-update) | async-done | bytes 1048592 | tf_op jit(solution)/shard_map/all_gather | solution.py:55
  400.5 210.0 %all-gather.8.cloned.1.call-done = bf16[1024,832]{1,0:T(8,128)(2,1)} async-done(((bf16[32,832]{1,0:T(8,128)(2,1)}), bf16[1024,832]{1,0:T(8,128)(2,1)}) %all-gather.8.cloned.1.call-update) | async-done | bytes 1703952 | tf_op jit(solution)/shard_map/all_gather | solution.py:70
  610.6 3.8 fusion
  614.4 222.3 %all-gather.10.cloned.1.call-done = bf16[1024,832]{1,0:T(8,128)(2,1)} async-done(((bf16[32,832]{1,0:T(8,128)(2,1)}), bf16[1024,832]{1,0:T(8,128)(2,1)}) %all-gather.10.cloned.1.call-update) | async-done | bytes 1703952 | tf_op jit(solution)/shard_map/all_gather | solution.py:71
  836.7 3.8 fusion.1
  840.6 1.2 fusion.19
  842.3 2.2 add_convert_fusion
  844.6 76.8 %reduce-scatter.11.cloned.1.call-done = bf16[416,512]{1,0:T(8,128)(2,1)} async-done(((bf16[832,512]{1,0:T(8,128)(2,1)}), bf16[416,512]{1,0:T(8,128)(2,1)}) %reduce-scatter.11.cloned.1.call-update) | async-done | bytes 426000 | tf_op jit(solution)/shard_map/reduce_scatter | solution.py:91
  921.4 60.5 %reduce-scatter.7.cloned.1.call-done = bf16[256,832]{0,1:T(8,128)(2,1)} async-done(((bf16[512,832]{0,1:T(8,128)(2,1)}), bf16[256,832]{0,1:T(8,128)(2,1)}) %reduce-scatter.7.cloned.1.call-update) | async-done | bytes 426000 | tf_op jit(solution)/shard_map/reduce_scatter | solution.py:85
  981.9 60.6 %reduce-scatter.9.cloned.1.call-done = bf16[256,832]{0,1:T(8,128)(2,1)} async-done(((bf16[512,832]{0,1:T(8,128)(2,1)}), bf16[256,832]{0,1:T(8,128)(2,1)}) %reduce-scatter.9.cloned.1.call-update) | async-done | bytes 426000 | tf_op jit(solution)/shard_map/reduce_scatter | solution.py:88
  1042.5 35.4 %reduce-scatter.5.cloned.1.call-done = bf16[128,512]{1,0:T(8,128)(2,1)} async-done(((bf16[1024,512]{1,0:T(8,128)(2,1)}), bf16[128,512]{1,0:T(8,128)(2,1)}) %reduce-scatter.5.cloned.1.call-update) | async-done | bytes 131088 | tf_op jit(solution)/shard_map/reduce_scatter | solution.py:74
  (35 shorter events, 2.8 us)
Async XLA Ops:
  7.2 38.4 %copy-start = (bf16[832,512]{1,0:T(8,128)(2,1)S(1)}, bf16[832,512]{1,0:T(8,128)(2,1)}, u32[]{:S(2)}) copy-start(bf16[832,512]{1,0:T(8,128)(2,1)} %param.17) | copy-start | bytes 2555908
  7.2 38.4 %all-gather.6.cloned.1.call-start = ((), (), s32[]{:S(2)}) async-start(), calls=%async_computation.5 | async-start | bytes 1179648 | tf_op jit(solution)/shard_map/all_gather | solution.py:56
  7.9 343.3 %all-gather.14.cloned.1.call-start = ((), (), s32[]{:S(2)}) async-start(), calls=%async_computation.12 | async-start | bytes 1892352 | tf_op jit(solution)/shard_map/all_gather | solution.py:72
  148.1 0.8 copy-start.1
  148.1 0.8 copy-start.2
  148.1 203.1 %copy-start.5 = (bf16[1024,512]{1,0:T(8,128)(2,1)S(1)}, bf16[1024,512]{1,0:T(8,128)(2,1)}, u32[]{:S(2)}) copy-start(bf16[1024,512]{1,0:T(8,128)(2,1)} %all-gather.6.cloned.1.call-done) | copy-start | bytes 3145732
  149.7 250.9 %all-gather.12.cloned.1.call-start = ((), (), s32[]{:S(2)}) async-start(), calls=%async_computation.9 | async-start | bytes 1179648 | tf_op jit(solution)/shard_map/all_gather | solution.py:55
  150.4 460.2 %all-gather.8.cloned.1.call-start = ((), (), s32[]{:S(2)}) async-start(), calls=%async_computation.6 | async-start | bytes 1892352 | tf_op jit(solution)/shard_map/all_gather | solution.py:70
  151.0 685.7 %all-gather.10.cloned.1.call-start = ((), (), s32[]{:S(2)}) async-start(), calls=%async_computation.7 | async-start | bytes 1892352 | tf_op jit(solution)/shard_map/all_gather | solution.py:71
  151.6 769.8 %reduce-scatter.11.cloned.1.call-start = ((), (), s32[]{:S(2)}) async-start(), calls=%async_computation.13 | async-start | bytes 1277952 | tf_op jit(solution)/shard_map/reduce_scatter | solution.py:91
  354.8 627.1 %reduce-scatter.7.cloned.1.call-start = ((), (), s32[]{:S(2)}) async-start(), calls=%async_computation.10 | async-start | bytes 1277952 | tf_op jit(solution)/shard_map/reduce_scatter | solution.py:85
  614.4 226.2 %copy-start.3 = (bf16[1024,832]{1,0:T(8,128)(2,1)S(1)}, bf16[1024,832]{1,0:T(8,128)(2,1)}, u32[]{:S(2)}) copy-start(bf16[1024,832]{1,0:T(8,128)(2,1)} %all-gather.8.cloned.1.call-done) | copy-start | bytes 5111812
  614.4 226.2 %copy-start.6 = (bf16[512,832]{0,1:T(8,128)(2,1)S(1)}, bf16[512,832]{0,1:T(8,128)(2,1)}, u32[]{:S(2)}) copy-start(bf16[512,832]{0,1:T(8,128)(2,1)} %param.15) | copy-start | bytes 2555908
  614.4 428.1 %reduce-scatter.9.cloned.1.call-start = ((), (), s32[]{:S(2)}) async-start(), calls=%async_computation.11 | async-start | bytes 1277952 | tf_op jit(solution)/shard_map/reduce_scatter | solution.py:88
  840.6 237.3 %reduce-scatter.5.cloned.1.call-start = ((), (), s32[]{:S(2)}) async-start(), calls=%async_computation.8 | async-start | bytes 1179648 | tf_op jit(solution)/shard_map/reduce_scatter | solution.py:74
  840.6 1.5 copy-start.4
  840.6 1.7 copy-start.7
Sparse Core Ops, SparseCore 0:
  10.1 35.3 all-gather.5
  149.8 201.3 all-gather.13
  353.4 47.0 all-gather.11
  403.0 207.4 all-gather.7
  613.1 223.6 all-gather.9
  840.0 81.3 reduce-scatter.10
  924.8 57.0 reduce-scatter.6
  985.3 57.1 reduce-scatter.8
  1045.9 31.9 reduce-scatter.4
where the time goes:
time: 1080 us
  waiting for transfers between devices  945 us (88%)
  blocking collectives  95.9 us (9%)
  matrix products  18.2 us (2%)
  between operations  13.9 us (1%)
    all_gather x1, waiting for transfers between devices, on_device(): lax.all_gather(part_up, 'col', axis=0, tiled=True)  222 us
    all_gather x1, waiting for transfers between devices, on_device(): lax.all_gather(part_gate, 'col', axis=0, tiled=True)  210 us
    all_gather x1, waiting for transfers between devices, on_device(): lax.all_gather(part_hidden, 'col', axis=0, tiled=True)  200 us
    all_to_all x1, blocking collectives, on_device(): lax.all_to_all(block_term, 'col', split_axis=0, concat_axis=0, tiled=True)  95.9 us
    reduce_scatter x1, waiting for transfers between devices, on_device(): lax.psum_scatter(down_term.astype(jnp.bfloat16), 'dp', scatter_dimension=...  76.8 us
    reduce_scatter x1, waiting for transfers between devices, on_device(): lax.psum_scatter(up_term.astype(jnp.bfloat16), 'dp', scatter_dimension=0,...  60.6 us
    reduce_scatter x1, waiting for transfers between devices, on_device(): lax.psum_scatter(gate_term.astype(jnp.bfloat16), 'dp', scatter_dimension=...  60.5 us
    all_gather x1, waiting for transfers between devices, on_device(): lax.all_gather(activations, 'row', axis=0, tiled=True)  45.7 us
  transfers between devices with their start and end apart: 9, of which 9 were waited for; matrix products, arithmetic and copies ran while one was open for 2% of the time, Pallas kernels for 0%

commit v1 on v0

--- a/solution.py
+++ b/solution.py
@@ -68,7 +68,9 @@
     part_gate, part_up, part_hidden = swiglu_grads(head_grad, gate_saved, up_saved)
     grad_gate, grad_up, hidden = (
         lax.all_gather(part_gate, "col", axis=0, tiled=True),
-        lax.all_gather(part_up, "col", axis=0, tiled=True),
+        jnp.concatenate(
+            lax.all_to_all(jnp.stack([part_up] * lax.axis_size("col")), "col", 0, 0), axis=0
+        ),
         lax.all_gather(part_hidden, "col", axis=0, tiled=True),
     )
     input_grad = lax.psum_scatter(

time: 1080 us -> 872 us (0.81)
  waiting for transfers between devices: 945 us -> 721 us
    all_gather x1 -> x0, waiting for transfers between devices: 222 us -> none  [on_device(): lax.all_gather(part_up, 'col', axis=0, tiled=True)]
    all_gather x1, waiting for transfers between devices: 200 us -> 211 us  [on_device(): lax.all_gather(part_hidden, 'col', axis=0, tiled=True)]
  transfers between devices with their start and end apart: 9 -> 9, of which waited for: 9 -> 8; matrix products, arithmetic and copies ran while one was open for 2% -> 3% of each run, Pallas kernels for 0% -> 0%
where the time goes in v1:
time: 872 us; the launch traced here: 871 us
  waiting for transfers between devices  721 us (83%)
  blocking collectives  95.9 us (11%)
  matrix products  19.6 us (2%)
  between operations  14.2 us (2%)
  starting transfers between devices  8.77 us (1%)
    all_gather x1, waiting for transfers between devices, on_device(): lax.all_gather(part_hidden, 'col', axis=0, tiled=True)  211 us
    all_gather x1, waiting for transfers between devices, on_device(): lax.all_gather(part_gate, 'col', axis=0, tiled=True)  210 us
    all_to_all x1, blocking collectives, on_device(): lax.all_to_all(block_term, 'col', split_axis=0, concat_axis=0, tiled=True)  95.9 us
    reduce_scatter x1, waiting for transfers between devices, on_device(): lax.psum_scatter(down_term.astype(jnp.bfloat16), 'dp', scatter_dimension=...  72.3 us
    reduce_scatter x1, waiting for transfers between devices, on_device(): lax.psum_scatter(up_term.astype(jnp.bfloat16), 'dp', scatter_dimension=0,...  60.6 us
    reduce_scatter x1, waiting for transfers between devices, on_device(): lax.psum_scatter(gate_term.astype(jnp.bfloat16), 'dp', scatter_dimension=...  60.4 us
    all_gather x1, waiting for transfers between devices, on_device(): lax.all_gather(activations, 'row', axis=0, tiled=True)  37.7 us
    reduce_scatter x1, waiting for transfers between devices, on_device(): lax.psum_scatter((contract_last(grad_gate, w_gate) + contract_last(grad_u...  35.3 us
  transfers between devices with their start and end apart: 9, of which 8 were waited for; matrix products, arithmetic and copies ran while one was open for 3% of the time, Pallas kernels for 0%

profile of v1, /device:TPU:2, one launch (start us, length us, event | category | flops | bytes accessed | tf_op | source)
XLA Modules:
  0.0 871.3 jit_solution(2708116155343189600)
XLA Ops:
  7.2 0.7 all-gather.5.cloned.1.call-update
  8.0 0.8 select_reduce_fusion.1
  8.8 0.8 select_reduce_fusion
  10.3 3.3 fusion.10
  13.6 32.0 %all-gather.5.cloned.1.call-done = bf16[1024,512]{1,0:T(8,128)(2,1)} async-done(((bf16[128,512]{1,0:T(8,128)(2,1)}), bf16[1024,512]{1,0:T(8,128)(2,1)}) %all-gather.5.cloned.1.call-update) | async-done | bytes 1048592 | tf_op jit(solution)/shard_map/all_gather | solution.py:56
  45.6 3.6 convolution_convert_fusion
  49.2 3.0 copy.14
  52.2 95.9 %all_to_all.14 = bf16[32,32,832]{2,1,0:T(8,128)(2,1)S(1)} all-to-all(bf16[32,32,832]{2,1,0:T(8,128)(2,1)S(1)} %bitcast.20), channel_id=1, replica_groups=mesh['dp'=2,'row'=8,'col'=32] {'col'}, dimensions={0} | all-to-all | bytes 3407872 | tf_op jit(solution)/shard_map/all_to_all | solution.py:65
  148.9 0.7 multiply_convert_fusion.3
  149.7 0.7 all-gather.9.cloned.1.call-update
  150.4 1.4 stack.2
  151.8 8.4 all-to-all-start.1
  160.9 210.9 %all-gather.11.cloned.1.call-done = bf16[1024,832]{1,0:T(8,128)(2,1)} async-done(((bf16[32,832]{1,0:T(8,128)(2,1)}), bf16[1024,832]{1,0:T(8,128)(2,1)}) %all-gather.11.cloned.1.call-update) | async-done | bytes 1703952 | tf_op jit(solution)/shard_map/all_gather | solution.py:74
  371.8 3.9 multiply_convert_fusion
  375.8 37.7 %all-gather.9.cloned.1.call-done = bf16[1024,512]{1,0:T(8,128)(2,1)} async-done(((bf16[128,512]{1,0:T(8,128)(2,1)}), bf16[1024,512]{1,0:T(8,128)(2,1)}) %all-gather.9.cloned.1.call-update) | async-done | bytes 1048592 | tf_op jit(solution)/shard_map/all_gather | solution.py:55
  413.5 210.0 %all-gather.7.cloned.1.call-done = bf16[1024,832]{1,0:T(8,128)(2,1)} async-done(((bf16[32,832]{1,0:T(8,128)(2,1)}), bf16[1024,832]{1,0:T(8,128)(2,1)}) %all-gather.7.cloned.1.call-update) | async-done | bytes 1703952 | tf_op jit(solution)/shard_map/all_gather | solution.py:70
  623.5 3.8 fusion
  627.4 3.3 fusion.1
  630.8 2.8 fusion.19
  633.7 2.2 add_convert_fusion
  635.9 72.3 %reduce-scatter.11.cloned.1.call-done = bf16[416,512]{1,0:T(8,128)(2,1)} async-done(((bf16[832,512]{1,0:T(8,128)(2,1)}), bf16[416,512]{1,0:T(8,128)(2,1)}) %reduce-scatter.11.cloned.1.call-update) | async-done | bytes 426000 | tf_op jit(solution)/shard_map/reduce_scatter | solution.py:93
  708.2 60.4 %reduce-scatter.7.cloned.1.call-done = bf16[256,832]{0,1:T(8,128)(2,1)} async-done(((bf16[512,832]{0,1:T(8,128)(2,1)}), bf16[256,832]{0,1:T(8,128)(2,1)}) %reduce-scatter.7.cloned.1.call-update) | async-done | bytes 426000 | tf_op jit(solution)/shard_map/reduce_scatter | solution.py:87
  768.5 60.6 %reduce-scatter.9.cloned.1.call-done = bf16[256,832]{0,1:T(8,128)(2,1)} async-done(((bf16[512,832]{0,1:T(8,128)(2,1)}), bf16[256,832]{0,1:T(8,128)(2,1)}) %reduce-scatter.9.cloned.1.call-update) | async-done | bytes 426000 | tf_op jit(solution)/shard_map/reduce_scatter | solution.py:90
  829.2 35.3 %reduce-scatter.5.cloned.1.call-done = bf16[128,512]{1,0:T(8,128)(2,1)} async-done(((bf16[1024,512]{1,0:T(8,128)(2,1)}), bf16[128,512]{1,0:T(8,128)(2,1)}) %reduce-scatter.5.cloned.1.call-update) | async-done | bytes 131088 | tf_op jit(solution)/shard_map/reduce_scatter | solution.py:76
  (29 shorter events, 2.4 us)
Async XLA Ops:
  7.2 38.4 %copy-start = (bf16[832,512]{1,0:T(8,128)(2,1)S(1)}, bf16[832,512]{1,0:T(8,128)(2,1)}, u32[]{:S(2)}) copy-start(bf16[832,512]{1,0:T(8,128)(2,1)} %param.17) | copy-start | bytes 2555908
  7.2 38.4 %all-gather.5.cloned.1.call-start = ((), (), s32[]{:S(2)}) async-start(), calls=%async_computation.6 | async-start | bytes 1179648 | tf_op jit(solution)/shard_map/all_gather | solution.py:56
  7.9 363.9 %all-gather.11.cloned.1.call-start = ((), (), s32[]{:S(2)}) async-start(), calls=%async_computation.12 | async-start | bytes 1892352 | tf_op jit(solution)/shard_map/all_gather | solution.py:74
  148.1 0.8 copy-start.1
  148.1 0.8 copy-start.2
  149.7 263.8 %all-gather.9.cloned.1.call-start = ((), (), s32[]{:S(2)}) async-start(), calls=%async_computation.9 | async-start | bytes 1179648 | tf_op jit(solution)/shard_map/all_gather | solution.py:55
  151.8 475.6 %all-to-all-start.1 = ((bf16[32,32,832]{2,1,0:T(8,128)(2,1)}), bf16[32,32,832]{2,1,0:T(8,128)(2,1)S(1)}, u32[]{:S(2)}, u32[]{:S(2)}) async-start(bf16[32,32,832]{2,1,0:T(8,128)(2,1)} %stack.2), calls=%async_computation.1 | async-start | bytes 3670016 | tf_op jit(solution)/shard_map/all_to_all | solution.py:72
  160.3 463.3 %all-gather.7.cloned.1.call-start = ((), (), s32[]{:S(2)}) async-start(), calls=%async_computation.7 | async-start | bytes 1892352 | tf_op jit(solution)/shard_map/all_gather | solution.py:70
  160.9 547.3 %reduce-scatter.11.cloned.1.call-start = ((), (), s32[]{:S(2)}) async-start(), calls=%async_computation.13 | async-start | bytes 1277952 | tf_op jit(solution)/shard_map/reduce_scatter | solution.py:93
  375.7 392.8 %reduce-scatter.7.cloned.1.call-start = ((), (), s32[]{:S(2)}) async-start(), calls=%async_computation.10 | async-start | bytes 1277952 | tf_op jit(solution)/shard_map/reduce_scatter | solution.py:87
  627.3 201.8 %reduce-scatter.9.cloned.1.call-start = ((), (), s32[]{:S(2)}) async-start(), calls=%async_computation.11 | async-start | bytes 1277952 | tf_op jit(solution)/shard_map/reduce_scatter | solution.py:90
  627.4 3.4 copy-start.3
  630.8 233.7 %reduce-scatter.5.cloned.1.call-start = ((), (), s32[]{:S(2)}) async-start(), calls=%async_computation.8 | async-start | bytes 1179648 | tf_op jit(solution)/shard_map/reduce_scatter | solution.py:76
  630.8 2.8 copy-start.4
Sparse Core Ops, SparseCore 0:
  10.1 35.3 all-gather.4
  149.8 221.9 all-gather.10
  374.0 39.4 all-gather.8
  416.0 207.4 all-gather.6
  626.8 81.3 reduce-scatter.10
  711.4 57.0 reduce-scatter.6
  771.9 57.1 reduce-scatter.8
  832.5 31.8 reduce-scatter.4
